TPU v7x, 512 devices: a whole 4x8x8 slice. The times are simulated.
512 devices in a mesh: centre: 16 (over y, core), sample: 32 (over z, x).
Axes of the slice: x: 4, y: 8, z: 8, core: 2. Of those that a mesh axis runs over, the one named last changes fastest.
Arguments:
- centres: bfloat16 [1024, 32768], P(None, 'centre'), may hold values from -40 to 40
- pool: bfloat16 [1024, 32768], P('centre', 'sample'), may hold values from -40 to 40
- labels: int32 [32768], P('sample'), may hold values from 0 to 143
- picks: int32 [2, 16384], P(None, 'sample'), may hold values from 0 to 32767, as said below
- coefs: float32 [144, 32768], P(None, ('centre', 'sample')), may hold values from -192 to 1024000
Outputs:
- new_coefs: float32 [144, 32768], P(None, ('centre', 'sample'))
Inputs may be any that keep to these rules, and one draw needn't show every extreme that they name: `picks`: entry b of a step's batch is a pool column in [(b // 512) * 1024, (b // 512 + 1) * 1024); entries may repeat.
All inputs are finite; a program needn't handle non-finite values.
Results may differ from a plain program's by a relative error of at most 0.00065.
Values may be sent and summed in bfloat16 or wider, within the bound.
No kernel may reach another device: no remote copies, remote signals or barrier semaphores. Data moves between devices by JAX's collectives and lax.ppermute only.
A program may use at most 64 MiB of HBM per device.

v0:
```python
import jax
import jax.numpy as jnp
from jax import lax
from jax.sharding import PartitionSpec as P

STEPS = 2
LOGIT_GAIN = 16.0
LENGTH_SCALE = 0.5
STEP_GAIN = 2048.0
EPS = 1e-06


def from_everyone(array, axis):
    peers = lax.axis_size(axis)
    return lax.all_to_all(
        jnp.broadcast_to(array[None], (peers, *array.shape)), axis, 0, 0, tiled=True
    )


def joined_along(parts, dim):
    dims = list(parts.shape[1:])
    dims[dim] *= parts.shape[0]
    return jnp.moveaxis(parts, 0, dim).reshape(dims)


def collect(array, axis, dim):
    parts = from_everyone(array, axis)
    return joined_along(parts, dim)


def over_pieces(array, axis):
    return lax.all_gather(array, axis).sum(0)


def cut_along(array, dim, peers):
    dims = array.shape
    parts = array.reshape(*dims[:dim], peers, dims[dim] // peers, *dims[dim + 1 :])
    return jnp.moveaxis(parts, dim, 0)


def summed_on_arrival(array, axis, dim):
    peers = lax.axis_size(axis)
    parts = lax.all_to_all(cut_along(array, dim, peers), axis, 0, 0, tiled=True)
    return jnp.sum(parts, axis=0)


def laplace(cross, sample_sq, centre_sq, width):
    mean_sq = (sample_sq[:, None] + centre_sq[None, :] - 2.0 * cross) / width
    return jnp.exp(-jnp.sqrt(mean_sq + EPS) / LENGTH_SCALE).astype(jnp.bfloat16)


def on_device(centres, pool, labels, picks, coefs):
    width = centres.shape[0]
    cen_dev = centres.shape[1]
    pool_dev = pool.shape[1]
    batch_dev = picks.shape[1]
    classes = coefs.shape[0]
    total_centres = cen_dev * lax.axis_size("centre")
    total_batch = batch_dev * lax.axis_size("sample")
    rate = STEP_GAIN * LOGIT_GAIN / total_batch
    centre_sq = jnp.sum(jnp.square(centres.astype(jnp.float32)), axis=0)
    local_picks = picks - lax.axis_index("sample") * pool_dev
    current = coefs
    for step in range(STEPS):
        coef_half = collect(current.astype(jnp.bfloat16), "sample", 1)
        chosen = local_picks[step]
        feats = jnp.take(pool, chosen, axis=1)
        labs = jnp.take(labels, chosen)
        gathered = lax.all_gather(feats, "centre", axis=0, tiled=True)
        cross = lax.dot_general(
            gathered, centres, (((0,), (0,)), ((), ())), preferred_element_type=jnp.float32
        )
        sample_sq = jnp.sum(jnp.square(gathered.astype(jnp.float32)), axis=0)
        kern = laplace(cross, sample_sq, centre_sq, width)
        partial_logits = lax.dot_general(
            coef_half, kern, (((1,), (1,)), ((), ())), preferred_element_type=jnp.float32
        )
        logits = over_pieces(partial_logits, "centre") * (LOGIT_GAIN / total_centres)
        top = jnp.max(logits, axis=0, keepdims=True)
        expo = jnp.exp(logits - top)
        probs = expo / jnp.sum(expo, axis=0, keepdims=True)
        class_ids = jnp.arange(classes, dtype=jnp.int32)
        onehot = (class_ids[:, None] == labs[None, :]).astype(jnp.float32)
        resid = (probs - onehot).astype(jnp.bfloat16)
        grad_part = jnp.dot(resid, kern, preferred_element_type=jnp.float32)
        current = current - rate * summed_on_arrival(grad_part, "sample", 1)
    return current


def solution(mesh):
    placed = (
        P(None, "centre"),
        P("centre", "sample"),
        P("sample"),
        P(None, "sample"),
        P(None, ("centre", "sample")),
    )
    return jax.shard_map(
        on_device,
        mesh=mesh,
        in_specs=placed,
        out_specs=P(None, ("centre", "sample")),
        check_vma=False,
    )
```

profile of v0, /device:TPU:2, one launch (start us, length us, event | category | flops | bytes accessed | tf_op | source)
XLA Modules:
  0.0 336.5 jit_solution(12417494301291164431)
XLA Ops:
  6.5 0.7 broadcast_subtract_fusion
  7.3 2.3 gather_fusion.1
  9.6 1.1 copy.40
  10.7 1.3 gather_fusion
  12.0 0.1 select_bitcast_fusion.1
  12.2 0.7 copy.41
  12.9 0.0 all-gather.7.cloned.1.call-update
  12.9 0.8 convert_element_type.36
  13.8 1.2 broadcast_in_dim.19
  14.9 13.5 %all-to-all-start = ((bf16[32,144,64]{1,2,0:T(8,128)(2,1)}), bf16[32,144,64]{1,2,0:T(8,128)(2,1)S(1)}, u32[]{:S(2)}, u32[]{:S(2)}) async-start(bf16[32,144,64]{1,2,0:T(8,128)(2,1)} %broadcast_in_dim.19), calls=%async_computation | async-start | bytes 2097152 | tf_op jit(solution)/shard_map/all_to_all | solution.py:15
  28.4 0.0 all-gather.11.cloned.1.call-start
  28.4 3.1 multiply_reduce_fusion
  31.5 27.1 %all-gather.7.cloned.1.call-done = bf16[1024,512]{1,0:T(8,128)(2,1)} async-done(((bf16[64,512]{1,0:T(8,128)(2,1)}), bf16[1024,512]{1,0:T(8,128)(2,1)}) %all-gather.7.cloned.1.call-update) | async-done | bytes 1048592 | tf_op jit(solution)/shard_map/all_gather | solution.py:69
  58.6 1.5 multiply_reduce_fusion.2
  60.1 6.8 %exponential_convert_fusion.1 = bf16[512,2048]{1,0:T(8,128)(2,1)S(1)} fusion(bf16[1024,512]{1,0:T(8,128)(2,1)} %all-gather.7.cloned.1.call-done, bf16[1024,2048]{1,0:T(8,128)(2,1)} %param.9, f32[2048]{0:T(1024)S(1)} %multiply_reduce_fusion, f32[512]{0:T(512)S(1)} %multiply_reduce_fusion.2), kind=kOutput, calls=%fused_computation.6 | convolution fusion | flops 2155872256 | bytes 7350272 | tf_op jit(solution)/shard_map/dot_general | solution.py:70
  66.9 1.6 convolution_bitcast_fusion
  68.4 0.0 all-gather.11.cloned.1.call-update
  68.4 44.5 %all-gather.11.cloned.1.call-done = f32[2304,512]{1,0:T(8,128)} async-done(((f32[144,512]{1,0:T(8,128)}), f32[2304,512]{1,0:T(8,128)}) %all-gather.11.cloned.1.call-update) | async-done | bytes 4718608 | tf_op jit(solution)/shard_map/all_gather | solution.py:32
  113.0 2.9 reduce_sum.83
  115.9 0.1 fusion
  116.0 1.6 fusion.2
  117.5 2.1 reshape.34
  119.6 2.4 copy.43
  122.0 10.6 %all-to-all-start.1 = ((f32[32,144,64]{1,2,0:T(8,128)}), f32[32,144,64]{1,2,0:T(8,128)S(1)}, u32[]{:S(2)}, u32[]{:S(2)}) async-start(f32[32,144,64]{1,2,0:T(8,128)} %copy.43), calls=%async_computation.1 | async-start | bytes 4194304 | tf_op jit(solution)/shard_map/all_to_all | solution.py:43
  132.7 0.0 all-gather.9.cloned.1.call-start
  132.7 2.3 gather_fusion.3
  135.0 1.3 gather_fusion.2
  136.4 0.1 select_bitcast_fusion
  136.6 0.7 copy.48
  137.3 45.0 %all-to-all-done.1 = f32[32,144,64]{1,2,0:T(8,128)S(1)} async-done(((f32[32,144,64]{1,2,0:T(8,128)}), f32[32,144,64]{1,2,0:T(8,128)S(1)}, u32[]{:S(2)}, u32[]{:S(2)}) %all-to-all-start.1) | async-done | bytes 1179680 | tf_op jit(solution)/shard_map/all_to_all | solution.py:43
  182.3 0.1 reduce_sum.85
  182.5 1.1 broadcast_in_dim.20
  183.6 6.5 %all-to-all-start.2 = ((bf16[32,144,64]{1,2,0:T(8,128)(2,1)}), bf16[32,144,64]{1,2,0:T(8,128)(2,1)S(1)}, u32[]{:S(2)}, u32[]{:S(2)}) async-start(bf16[32,144,64]{1,2,0:T(8,128)(2,1)} %broadcast_in_dim.20), calls=%async_computation.2 | async-start | bytes 2097152 | tf_op jit(solution)/shard_map/all_to_all | solution.py:15
  190.1 0.0 all-gather.13.cloned.1.call-start
  190.1 0.0 all-gather.9.cloned.1.call-done
  190.2 1.5 multiply_reduce_fusion.1
  191.7 6.7 %exponential_convert_fusion = bf16[512,2048]{1,0:T(8,128)(2,1)S(1)} fusion(bf16[1024,512]{1,0:T(8,128)(2,1)} %all-gather.9.cloned.1.call-done, bf16[1024,2048]{1,0:T(8,128)(2,1)} %param.9, f32[512]{0:T(512)S(1)} %multiply_reduce_fusion.1, f32[2048]{0:T(1024)S(1)} %multiply_reduce_fusion), kind=kOutput, calls=%fused_computation.5 | convolution fusion | flops 2155872256 | bytes 7350272 | tf_op jit(solution)/shard_map/dot_general | solution.py:70
  198.4 19.8 %all-to-all-done.2 = bf16[32,144,64]{1,2,0:T(8,128)(2,1)S(1)} async-done(((bf16[32,144,64]{1,2,0:T(8,128)(2,1)}), bf16[32,144,64]{1,2,0:T(8,128)(2,1)S(1)}, u32[]{:S(2)}, u32[]{:S(2)}) %all-to-all-start.2) | async-done | bytes 589856 | tf_op jit(solution)/shard_map/all_to_all | solution.py:15
  218.2 1.6 fusion.16
  219.8 39.4 %all-gather.13.cloned.1.call-done = f32[2304,512]{1,0:T(8,128)} async-done(((f32[144,512]{1,0:T(8,128)}), f32[2304,512]{1,0:T(8,128)}) %all-gather.13.cloned.1.call-update) | async-done | bytes 4718608 | tf_op jit(solution)/shard_map/all_gather | solution.py:32
  259.2 2.9 reduce_sum.87
  262.1 0.1 fusion.1
  262.1 2.1 fusion.3
  264.3 0.9 reshape.36
  265.2 2.4 copy.49
  267.6 61.6 %all_to_all.20 = f32[32,144,64]{1,2,0:T(8,128)S(1)} all-to-all(f32[32,144,64]{1,2,0:T(8,128)} %copy.49), channel_id=1, replica_groups=mesh['centre'=16,'sample'=32] {'sample'}, dimensions={0} | all-to-all | bytes 2359296 | tf_op jit(solution)/shard_map/all_to_all | solution.py:43
  329.2 0.1 reduce_sum.89
  329.4 0.6 multiply_subtract_fusion
  (26 shorter events, 0.2 us)
Async XLA Ops:
  6.5 0.7 copy-start
  6.5 52.0 %all-gather.7.cloned.1.call-start = ((), (), s32[]{:S(2)}) async-start(), calls=%async_computation.4 | async-start | bytes 1114112 | tf_op jit(solution)/shard_map/all_gather | solution.py:69
  14.9 51.9 %all-to-all-start = ((bf16[32,144,64]{1,2,0:T(8,128)(2,1)}), bf16[32,144,64]{1,2,0:T(8,128)(2,1)S(1)}, u32[]{:S(2)}, u32[]{:S(2)}) async-start(bf16[32,144,64]{1,2,0:T(8,128)(2,1)} %broadcast_in_dim.19), calls=%async_computation | async-start | bytes 2097152 | tf_op jit(solution)/shard_map/all_to_all | solution.py:15
  28.4 84.6 %all-gather.11.cloned.1.call-start = ((), (), s32[]{:S(2)}) async-start(), calls=%async_computation.6 | async-start | bytes 5013504 | tf_op jit(solution)/shard_map/all_gather | solution.py:32
  122.0 60.4 %copy-start.4 = (f32[144,64]{0,1:T(8,128)S(1)}, f32[144,64]{0,1:T(8,128)}, u32[]{:S(2)}) copy-start(f32[144,64]{0,1:T(8,128)} %param.13) | copy-start | bytes 110596
  122.0 60.3 %all-to-all-start.1 = ((f32[32,144,64]{1,2,0:T(8,128)}), f32[32,144,64]{1,2,0:T(8,128)S(1)}, u32[]{:S(2)}, u32[]{:S(2)}) async-start(f32[32,144,64]{1,2,0:T(8,128)} %copy.43), calls=%async_computation.1 | async-start | bytes 4194304 | tf_op jit(solution)/shard_map/all_to_all | solution.py:43
  132.7 57.5 %all-gather.9.cloned.1.call-start = ((), (), s32[]{:S(2)}) async-start(), calls=%async_computation.5 | async-start | bytes 1114112 | tf_op jit(solution)/shard_map/all_gather | solution.py:69
  182.5 7.7 %copy-start.2 = (f32[144,64]{0,1:T(8,128)}, f32[144,64]{0,1:T(8,128)S(1)}, u32[]{:S(2)}) copy-start(f32[144,64]{0,1:T(8,128)S(1)} %reduce_sum.85) | copy-start | bytes 110596
  183.6 34.6 %all-to-all-start.2 = ((bf16[32,144,64]{1,2,0:T(8,128)(2,1)}), bf16[32,144,64]{1,2,0:T(8,128)(2,1)S(1)}, u32[]{:S(2)}, u32[]{:S(2)}) async-start(bf16[32,144,64]{1,2,0:T(8,128)(2,1)} %broadcast_in_dim.20), calls=%async_computation.2 | async-start | bytes 2097152 | tf_op jit(solution)/shard_map/all_to_all | solution.py:15
  190.1 69.1 %all-gather.13.cloned.1.call-start = ((), (), s32[]{:S(2)}) async-start(), calls=%async_computation.7 | async-start | bytes 5013504 | tf_op jit(solution)/shard_map/all_gather | solution.py:32
  198.4 60.7 %copy-start.1 = (bf16[512,2048]{1,0:T(8,128)(2,1)}, bf16[512,2048]{1,0:T(8,128)(2,1)S(1)}, u32[]{:S(2)}) copy-start(bf16[512,2048]{1,0:T(8,128)(2,1)S(1)} %exponential_convert_fusion) | copy-start | bytes 6291460
  267.6 61.7 %copy-start.3 = (f32[144,64]{0,1:T(8,128)S(1)}, f32[144,64]{0,1:T(8,128)}, u32[]{:S(2)}) copy-start(f32[144,64]{0,1:T(8,128)} %copy-done.2) | copy-start | bytes 110596
  267.6 61.7 %copy-start.5 = (f32[144,64]{0,1:T(8,128)S(1)}, f32[144,64]{0,1:T(8,128)}, u32[]{:S(2)}) copy-start(f32[144,64]{0,1:T(8,128)} %param.13) | copy-start | bytes 110596
Sparse Core Ops, SparseCore 0:
  13.0 45.5 all-gather.6
  68.6 44.3 all-gather.10
  137.4 38.9 all-gather.8
  219.9 39.2 all-gather.12
where the time goes:
time: 337 us
  waiting for transfers between devices  176 us (52%)
  blocking collectives  61.6 us (18%)
  starting transfers between devices  30.7 us (9%)
  matrix products  20.3 us (6%)
  local copies, waits for them, and re-layouts  19.9 us (6%)
  other arithmetic  14.8 us (4%)
  between operations  13.4 us (4%)
    all_gather x2, waiting for transfers between devices, over_pieces(): return lax.all_gather(array, axis).sum(0)  83.9 us
    all_to_all x1, blocking collectives, summed_on_arrival(): parts = lax.all_to_all(cut_along(array, dim, peers), axis, 0, 0, tiled=True)  61.6 us
    all_to_all x1, waiting for transfers between devices, summed_on_arrival(): parts = lax.all_to_all(cut_along(array, dim, peers), axis, 0, 0, tiled=True)  45 us
    all_gather x2, waiting for transfers between devices, on_device(): gathered = lax.all_gather(feats, 'centre', axis=0, tiled=True)  27.1 us
    all_to_all x2, starting transfers between devices, from_everyone(): lax.all_to_all(jnp.broadcast_to(array[None], (peers, *array.shape)), axis...  19.9 us
    all_to_all x2, waiting for transfers between devices, from_everyone(): lax.all_to_all(jnp.broadcast_to(array[None], (peers, *array.shape)), axis...  19.8 us
    dot_general x2, matrix products, on_device(): lax.dot_general(gathered, centres, (((0,), (0,)), ((), ())), preferred_el...  13.5 us
    all_to_all x1, starting transfers between devices, summed_on_arrival(): parts = lax.all_to_all(cut_along(array, dim, peers), axis, 0, 0, tiled=True)  10.6 us
  transfers between devices with their start and end apart: 7, of which 5 were waited for; matrix products, arithmetic and copies ran while one was open for 8% of the time, Pallas kernels for 0%

commit v1 on v0

--- a/solution.py
+++ b/solution.py
@@ -1,3 +1,4 @@
+import functools
 import jax
 import jax.numpy as jnp
 from jax import lax
@@ -8,6 +9,28 @@
 LENGTH_SCALE = 0.5
 STEP_GAIN = 2048.0
 EPS = 1e-06
+
+
+def choose_the_stops_all(matrix, named_axis):
+    n = lax.axis_size(named_axis)
+    runs = []
+    for dev in range(n):
+        runs.append((dev, (dev + 1) % n))
+    chunks = []
+    for dev in range(n):
+        chunks.append((dev, (dev - 1) % n))
+    small, q_next = ([matrix], [matrix])
+    for _ in range(n // 2):
+        small.append(lax.ppermute(small[-1], named_axis, runs))
+    for _ in range((n - 1) // 2):
+        row_out = lax.ppermute(q_next[-1], axis_name=named_axis, perm=chunks)
+        q_next.append(row_out)
+    item_now = jnp.concatenate([*small[::-1], *q_next[1:]], 0)
+    o_now = jnp.roll(item_now, (lax.axis_index(named_axis) - n // 2) * matrix.shape[0], 0)
+    return o_now
+
+
+take_copies_all = functools.partial(choose_the_stops_all, named_axis="centre")
 
 
 def from_everyone(array, axis):
@@ -66,7 +89,7 @@
         chosen = local_picks[step]
         feats = jnp.take(pool, chosen, axis=1)
         labs = jnp.take(labels, chosen)
-        gathered = lax.all_gather(feats, "centre", axis=0, tiled=True)
+        gathered = take_copies_all(feats)
         cross = lax.dot_general(
             gathered, centres, (((0,), (0,)), ((), ())), preferred_element_type=jnp.float32
         )

time: 337 us -> 367 us (1.089)
  starting transfers between devices: 30.7 us -> 71.5 us
  waiting for transfers between devices: 176 us -> 163 us
    ppermute x0 -> x30, starting transfers between devices: none -> 41 us  [the longest x14 41 us: choose_the_stops_all(): row_out = lax.ppermute(q_next[-1], axis_name=named_axis, perm=chunks)]
    ppermute x0 -> x30, waiting for transfers between devices: none -> 38.8 us  [the longest x16 28.5 us: choose_the_stops_all(): small.append(lax.ppermute(small[-1], named_axis, runs))]
    all_gather x2 -> x0, waiting for transfers between devices: 27.1 us -> none  [on_device(): gathered = lax.all_gather(feats, 'centre', axis=0, tiled=True)]
    all_to_all x1, waiting for transfers between devices: 45 us -> 29 us  [summed_on_arrival(): parts = lax.all_to_all(cut_along(array, dim, peers), axis, 0, 0, tiled=True)]
    all_to_all x2, waiting for transfers between devices: 19.8 us -> 7.3 us  [from_everyone(): lax.all_to_all(jnp.broadcast_to(array[None], (peers, *array.shape)), axis...]
    all_gather x2, waiting for transfers between devices: 83.9 us -> 88 us  [over_pieces(): return lax.all_gather(array, axis).sum(0)]
  transfers between devices with their start and end apart: 7 -> 35, of which waited for: 5 -> 20; matrix products, arithmetic and copies ran while one was open for 8% -> 7% of each run, Pallas kernels for 0% -> 0%
where the time goes in v1:
time: 367 us; the launch traced here: 366 us
  waiting for transfers between devices  163 us (44%)
  starting transfers between devices  71.5 us (19%)
  blocking collectives  61.5 us (17%)
  matrix products  22.9 us (6%)
  local copies, waits for them, and re-layouts  20.1 us (5%)
  between operations  13.7 us (4%)
  other arithmetic  13.5 us (4%)
    all_gather x2, waiting for transfers between devices, over_pieces(): return lax.all_gather(array, axis).sum(0)  88 us
    all_to_all x1, blocking collectives, summed_on_arrival(): parts = lax.all_to_all(cut_along(array, dim, peers), axis, 0, 0, tiled=True)  61.5 us
    ppermute x14, starting transfers between devices, choose_the_stops_all(): row_out = lax.ppermute(q_next[-1], axis_name=named_axis, perm=chunks)  41 us
    all_to_all x1, waiting for transfers between devices, summed_on_arrival(): parts = lax.all_to_all(cut_along(array, dim, peers), axis, 0, 0, tiled=True)  29 us
    ppermute x16, waiting for transfers between devices, choose_the_stops_all(): small.append(lax.ppermute(small[-1], named_axis, runs))  28.5 us
    all_to_all x2, starting transfers between devices, from_everyone(): lax.all_to_all(jnp.broadcast_to(array[None], (peers, *array.shape)), axis...  19.9 us
    dot_general x2, matrix products, on_device(): lax.dot_general(gathered, centres, (((0,), (0,)), ((), ())), preferred_el...  12.8 us
    all_to_all x1, starting transfers between devices, summed_on_arrival(): parts = lax.all_to_all(cut_along(array, dim, peers), axis, 0, 0, tiled=True)  10.5 us
  transfers between devices with their start and end apart: 35, of which 20 were waited for; matrix products, arithmetic and copies ran while one was open for 7% of the time, Pallas kernels for 0%

profile of v1, /device:TPU:2, one launch (start us, length us, event | category | flops | bytes accessed | tf_op | source)
XLA Modules:
  0.0 366.3 jit_solution(12091705410267244209)
XLA Ops:
  7.3 2.3 gather_fusion.1
  11.3 2.9 collective-permute-start.8
  14.3 2.6 collective-permute-done
  16.9 3.0 collective-permute-start.9
  19.9 2.6 collective-permute-done.1
  22.5 3.0 collective-permute-start.10
  25.5 2.6 collective-permute-done.2
  28.1 3.0 collective-permute-start.11
  31.1 2.6 collective-permute-done.3
  33.7 3.0 collective-permute-start.12
  36.7 2.6 collective-permute-done.4
  39.3 3.0 collective-permute-start.13
  42.3 2.6 collective-permute-done.5
  46.1 13.5 %all-to-all-start = ((bf16[32,144,64]{1,2,0:T(8,128)(2,1)}), bf16[32,144,64]{1,2,0:T(8,128)(2,1)}, u32[]{:S(2)}, u32[]{:S(2)}) async-start(bf16[32,144,64]{1,2,0:T(8,128)(2,1)} %broadcast_in_dim.19), calls=%async_computation | async-start | bytes 2097152 | tf_op jit(solution)/shard_map/all_to_all | solution.py:38
  59.6 2.4 collective-permute-start.14
  62.0 3.1 multiply_reduce_fusion
  65.1 2.5 collective-permute-done.7
  69.9 6.4 %exponential_convert_fusion.1 = bf16[512,2048]{1,0:T(8,128)(2,1)S(1)} fusion(bf16[1024,2048]{1,0:T(8,128)(2,1)} %param.11, f32[2048]{0:T(1024)S(1)} %multiply_reduce_fusion, f32[512]{0:T(512)S(1)} %multiply_reduce_fusion.2, s32[]{:T(128)S(6)} %select_n.34, bf16[1024,512]{0,1:T(8,128)(2,1)S(1)} %concatenate.9), kind=kOutput, calls=%fused_computation.6 | convolution fusion | flops 2157969408 | bytes 7350276 | tf_op jit(solution)/shard_map/dot_general | solution.py:93
  76.3 7.3 %all-to-all-done = bf16[32,144,64]{1,2,0:T(8,128)(2,1)} async-done(((bf16[32,144,64]{1,2,0:T(8,128)(2,1)}), bf16[32,144,64]{1,2,0:T(8,128)(2,1)}, u32[]{:S(2)}, u32[]{:S(2)}) %all-to-all-start) | async-done | bytes 589856 | tf_op jit(solution)/shard_map/all_to_all | solution.py:38
  83.6 2.8 convolution_bitcast_fusion
  86.4 44.3 %all-gather.5.cloned.1.call-done = f32[2304,512]{1,0:T(8,128)} async-done(((f32[144,512]{1,0:T(8,128)}), f32[2304,512]{1,0:T(8,128)}) %all-gather.5.cloned.1.call-update) | async-done | bytes 4718608 | tf_op jit(solution)/shard_map/all_gather | solution.py:55
  130.7 2.9 reduce_sum.83
  135.3 2.1 reshape.34
  137.4 2.4 copy.38
  139.7 10.5 %all-to-all-start.1 = ((f32[32,144,64]{1,2,0:T(8,128)}), f32[32,144,64]{1,2,0:T(8,128)S(1)}, u32[]{:S(2)}, u32[]{:S(2)}) async-start(f32[32,144,64]{1,2,0:T(8,128)} %copy.38), calls=%async_computation.1 | async-start | bytes 4194304 | tf_op jit(solution)/shard_map/all_to_all | solution.py:66
  150.3 2.3 gather_fusion.3
  154.1 2.9 collective-permute-start.23
  157.1 2.6 collective-permute-done.15
  159.7 3.2 collective-permute-start.24
  163.0 2.4 collective-permute-done.16
  165.5 3.4 collective-permute-start.25
  170.9 29.0 %all-to-all-done.1 = f32[32,144,64]{1,2,0:T(8,128)S(1)} async-done(((f32[32,144,64]{1,2,0:T(8,128)}), f32[32,144,64]{1,2,0:T(8,128)S(1)}, u32[]{:S(2)}, u32[]{:S(2)}) %all-to-all-start.1) | async-done | bytes 1179680 | tf_op jit(solution)/shard_map/all_to_all | solution.py:66
  201.2 6.4 %all-to-all-start.2 = ((bf16[32,144,64]{1,2,0:T(8,128)(2,1)}), bf16[32,144,64]{1,2,0:T(8,128)(2,1)}, u32[]{:S(2)}, u32[]{:S(2)}) async-start(bf16[32,144,64]{1,2,0:T(8,128)(2,1)} %broadcast_in_dim.20), calls=%async_computation.2 | async-start | bytes 2097152 | tf_op jit(solution)/shard_map/all_to_all | solution.py:38
  208.6 2.5 collective-permute-done.26
  211.1 3.3 collective-permute-start.27
  214.4 2.5 collective-permute-done.27
  217.0 3.5 collective-permute-start.28
  220.4 2.5 collective-permute-done.28
  223.0 3.5 collective-permute-start.29
  226.4 2.5 collective-permute-done.29
  229.0 3.1 collective-permute-done.22
  234.3 6.4 %exponential_convert_fusion = bf16[512,2048]{1,0:T(8,128)(2,1)S(1)} fusion(bf16[1024,2048]{1,0:T(8,128)(2,1)} %param.11, f32[512]{0:T(512)S(1)} %multiply_reduce_fusion.1, f32[2048]{0:T(1024)S(1)} %multiply_reduce_fusion, s32[]{:T(128)S(6)} %select_n.34, bf16[1024,512]{0,1:T(8,128)(2,1)S(1)} %concatenate.10), kind=kOutput, calls=%fused_computation.5 | convolution fusion | flops 2157969408 | bytes 7350276 | tf_op jit(solution)/shard_map/dot_general | solution.py:93
  240.7 3.6 fusion.20
  244.3 43.7 %all-gather.7.cloned.1.call-done = f32[2304,512]{1,0:T(8,128)} async-done(((f32[144,512]{1,0:T(8,128)}), f32[2304,512]{1,0:T(8,128)}) %all-gather.7.cloned.1.call-update) | async-done | bytes 4718608 | tf_op jit(solution)/shard_map/all_gather | solution.py:55
  288.1 2.9 reduce_sum.87
  291.1 2.1 fusion.5
  294.1 2.4 copy.43
  296.5 61.5 %all_to_all.20 = f32[32,144,64]{1,2,0:T(8,128)S(1)} all-to-all(f32[32,144,64]{1,2,0:T(8,128)} %copy.43), channel_id=1, replica_groups=mesh['centre'=16,'sample'=32] {'sample'}, dimensions={0} | all-to-all | bytes 2359296 | tf_op jit(solution)/shard_map/all_to_all | solution.py:66
  (82 shorter events, 18.5 us)
Async XLA Ops:
  6.5 0.8 copy-start
  6.5 3.1 copy-start.6
  6.5 38.4 %copy-start.4 = (f32[144,64]{0,1:T(8,128)S(1)}, f32[144,64]{0,1:T(8,128)}, u32[]{:S(2)}) copy-start(f32[144,64]{0,1:T(8,128)} %param.15) | copy-start | bytes 110596
  11.3 5.6 %collective-permute-start = (bf16[64,512]{0,1:T(8,128)(2,1)S(1)}, bf16[64,512]{0,1:T(8,128)(2,1)S(1)}, u32[]{:S(2)}, u32[]{:S(2)}) collective-permute-start(bf16[64,512]{0,1:T(8,128)(2,1)S(1)} %select_bitcast_fusion.1), channel_id=1, source_target_pairs={{0,32},{32,64},{64,96},{96,128},{128,160},{160,192},{192,224},{224... | collective-permute-start | bytes 196616 | tf_op jit(solution)/shard_map/ppermute | solution.py:24
  11.3 5.6 %collective-permute-start.8 = (bf16[64,512]{0,1:T(8,128)(2,1)S(1)}, bf16[64,512]{0,1:T(8,128)(2,1)S(1)}, u32[]{:S(2)}, u32[]{:S(2)}) collective-permute-start(bf16[64,512]{0,1:T(8,128)(2,1)S(1)} %select_bitcast_fusion.1), channel_id=1, source_target_pairs={{0,480},{32,0},{64,32},{96,64},{128,96},{160,128},{192,160},{224,1... | collective-permute-start | bytes 196616 | tf_op jit(solution)/shard_map/ppermute | solution.py:26
  16.9 5.6 %collective-permute-start.1 = (bf16[64,512]{0,1:T(8,128)(2,1)S(1)}, bf16[64,512]{0,1:T(8,128)(2,1)S(1)}, u32[]{:S(2)}, u32[]{:S(2)}) collective-permute-start(bf16[64,512]{0,1:T(8,128)(2,1)S(1)} %collective-permute-done), channel_id=1, source_target_pairs={{0,32},{32,64},{64,96},{96,128},{128,160},{160,192},{192,224},{224... | collective-permute-start | bytes 196616 | tf_op jit(solution)/shard_map/ppermute | solution.py:24
  16.9 5.6 %collective-permute-start.9 = (bf16[64,512]{0,1:T(8,128)(2,1)S(1)}, bf16[64,512]{0,1:T(8,128)(2,1)S(1)}, u32[]{:S(2)}, u32[]{:S(2)}) collective-permute-start(bf16[64,512]{0,1:T(8,128)(2,1)S(1)} %collective-permute-done.8), channel_id=1, source_target_pairs={{0,480},{32,0},{64,32},{96,64},{128,96},{160,128},{192,160},{224,1... | collective-permute-start | bytes 196616 | tf_op jit(solution)/shard_map/ppermute | solution.py:26
  22.5 5.6 %collective-permute-start.2 = (bf16[64,512]{0,1:T(8,128)(2,1)S(1)}, bf16[64,512]{0,1:T(8,128)(2,1)S(1)}, u32[]{:S(2)}, u32[]{:S(2)}) collective-permute-start(bf16[64,512]{0,1:T(8,128)(2,1)S(1)} %collective-permute-done.1), channel_id=1, source_target_pairs={{0,32},{32,64},{64,96},{96,128},{128,160},{160,192},{192,224},{224... | collective-permute-start | bytes 196616 | tf_op jit(solution)/shard_map/ppermute | solution.py:24
  22.5 5.6 %collective-permute-start.10 = (bf16[64,512]{0,1:T(8,128)(2,1)S(1)}, bf16[64,512]{0,1:T(8,128)(2,1)S(1)}, u32[]{:S(2)}, u32[]{:S(2)}) collective-permute-start(bf16[64,512]{0,1:T(8,128)(2,1)S(1)} %collective-permute-done.9), channel_id=1, source_target_pairs={{0,480},{32,0},{64,32},{96,64},{128,96},{160,128},{192,160},{224,1... | collective-permute-start | bytes 196616 | tf_op jit(solution)/shard_map/ppermute | solution.py:26
  28.1 5.6 %collective-permute-start.3 = (bf16[64,512]{0,1:T(8,128)(2,1)S(1)}, bf16[64,512]{0,1:T(8,128)(2,1)S(1)}, u32[]{:S(2)}, u32[]{:S(2)}) collective-permute-start(bf16[64,512]{0,1:T(8,128)(2,1)S(1)} %collective-permute-done.2), channel_id=1, source_target_pairs={{0,32},{32,64},{64,96},{96,128},{128,160},{160,192},{192,224},{224... | collective-permute-start | bytes 196616 | tf_op jit(solution)/shard_map/ppermute | solution.py:24
  28.1 5.6 %collective-permute-start.11 = (bf16[64,512]{0,1:T(8,128)(2,1)S(1)}, bf16[64,512]{0,1:T(8,128)(2,1)S(1)}, u32[]{:S(2)}, u32[]{:S(2)}) collective-permute-start(bf16[64,512]{0,1:T(8,128)(2,1)S(1)} %collective-permute-done.10), channel_id=1, source_target_pairs={{0,480},{32,0},{64,32},{96,64},{128,96},{160,128},{192,160},{224,1... | collective-permute-start | bytes 196616 | tf_op jit(solution)/shard_map/ppermute | solution.py:26
  33.7 5.6 %collective-permute-start.4 = (bf16[64,512]{0,1:T(8,128)(2,1)S(1)}, bf16[64,512]{0,1:T(8,128)(2,1)S(1)}, u32[]{:S(2)}, u32[]{:S(2)}) collective-permute-start(bf16[64,512]{0,1:T(8,128)(2,1)S(1)} %collective-permute-done.3), channel_id=1, source_target_pairs={{0,32},{32,64},{64,96},{96,128},{128,160},{160,192},{192,224},{224... | collective-permute-start | bytes 196616 | tf_op jit(solution)/shard_map/ppermute | solution.py:24
  33.7 5.6 %collective-permute-start.12 = (bf16[64,512]{0,1:T(8,128)(2,1)S(1)}, bf16[64,512]{0,1:T(8,128)(2,1)S(1)}, u32[]{:S(2)}, u32[]{:S(2)}) collective-permute-start(bf16[64,512]{0,1:T(8,128)(2,1)S(1)} %collective-permute-done.11), channel_id=1, source_target_pairs={{0,480},{32,0},{64,32},{96,64},{128,96},{160,128},{192,160},{224,1... | collective-permute-start | bytes 196616 | tf_op jit(solution)/shard_map/ppermute | solution.py:26
  39.3 5.6 %collective-permute-start.5 = (bf16[64,512]{0,1:T(8,128)(2,1)S(1)}, bf16[64,512]{0,1:T(8,128)(2,1)S(1)}, u32[]{:S(2)}, u32[]{:S(2)}) collective-permute-start(bf16[64,512]{0,1:T(8,128)(2,1)S(1)} %collective-permute-done.4), channel_id=1, source_target_pairs={{0,32},{32,64},{64,96},{96,128},{128,160},{160,192},{192,224},{224... | collective-permute-start | bytes 196616 | tf_op jit(solution)/shard_map/ppermute | solution.py:24
  39.3 20.3 %collective-permute-start.13 = (bf16[64,512]{0,1:T(8,128)(2,1)S(1)}, bf16[64,512]{0,1:T(8,128)(2,1)S(1)}, u32[]{:S(2)}, u32[]{:S(2)}) collective-permute-start(bf16[64,512]{0,1:T(8,128)(2,1)S(1)} %collective-permute-done.12), channel_id=1, source_target_pairs={{0,480},{32,0},{64,32},{96,64},{128,96},{160,128},{192,160},{224,1... | collective-permute-start | bytes 196616 | tf_op jit(solution)/shard_map/ppermute | solution.py:26
  44.9 17.1 %collective-permute-start.6 = (bf16[64,512]{0,1:T(8,128)(2,1)S(1)}, bf16[64,512]{0,1:T(8,128)(2,1)S(1)}, u32[]{:S(2)}, u32[]{:S(2)}) collective-permute-start(bf16[64,512]{0,1:T(8,128)(2,1)S(1)} %collective-permute-done.5), channel_id=1, source_target_pairs={{0,32},{32,64},{64,96},{96,128},{128,160},{160,192},{192,224},{224... | collective-permute-start | bytes 196616 | tf_op jit(solution)/shard_map/ppermute | solution.py:24
  46.1 37.6 %all-to-all-start = ((bf16[32,144,64]{1,2,0:T(8,128)(2,1)}), bf16[32,144,64]{1,2,0:T(8,128)(2,1)}, u32[]{:S(2)}, u32[]{:S(2)}) async-start(bf16[32,144,64]{1,2,0:T(8,128)(2,1)} %broadcast_in_dim.19), calls=%async_computation | async-start | bytes 2097152 | tf_op jit(solution)/shard_map/all_to_all | solution.py:38
  59.6 71.1 %all-gather.5.cloned.1.call-start = ((), (), s32[]{:S(2)}) async-start(), calls=%async_computation.4 | async-start | bytes 5013504 | tf_op jit(solution)/shard_map/all_gather | solution.py:55
  59.6 5.5 %collective-permute-start.14 = (bf16[64,512]{0,1:T(8,128)(2,1)S(1)}, bf16[64,512]{0,1:T(8,128)(2,1)S(1)}, u32[]{:S(2)}, u32[]{:S(2)}) collective-permute-start(bf16[64,512]{0,1:T(8,128)(2,1)S(1)} %collective-permute-done.13), channel_id=1, source_target_pairs={{0,480},{32,0},{64,32},{96,64},{128,96},{160,128},{192,160},{224,1... | collective-permute-start | bytes 196616 | tf_op jit(solution)/shard_map/ppermute | solution.py:26
  62.0 5.6 %collective-permute-start.7 = (bf16[64,512]{0,1:T(8,128)(2,1)S(1)}, bf16[64,512]{0,1:T(8,128)(2,1)S(1)}, u32[]{:S(2)}, u32[]{:S(2)}) collective-permute-start(bf16[64,512]{0,1:T(8,128)(2,1)S(1)} %collective-permute-done.6), channel_id=1, source_target_pairs={{0,32},{32,64},{64,96},{96,128},{128,160},{160,192},{192,224},{224... | collective-permute-start | bytes 196616 | tf_op jit(solution)/shard_map/ppermute | solution.py:24
  139.7 60.2 %all-to-all-start.1 = ((f32[32,144,64]{1,2,0:T(8,128)}), f32[32,144,64]{1,2,0:T(8,128)S(1)}, u32[]{:S(2)}, u32[]{:S(2)}) async-start(f32[32,144,64]{1,2,0:T(8,128)} %copy.38), calls=%async_computation.1 | async-start | bytes 4194304 | tf_op jit(solution)/shard_map/all_to_all | solution.py:66
  154.1 5.6 %collective-permute-start.15 = (bf16[64,512]{0,1:T(8,128)(2,1)S(1)}, bf16[64,512]{0,1:T(8,128)(2,1)S(1)}, u32[]{:S(2)}, u32[]{:S(2)}) collective-permute-start(bf16[64,512]{0,1:T(8,128)(2,1)S(1)} %select_bitcast_fusion), channel_id=1, source_target_pairs={{0,32},{32,64},{64,96},{96,128},{128,160},{160,192},{192,224},{224... | collective-permute-start | bytes 196616 | tf_op jit(solution)/shard_map/ppermute | solution.py:24
  154.1 5.6 %collective-permute-start.23 = (bf16[64,512]{0,1:T(8,128)(2,1)S(1)}, bf16[64,512]{0,1:T(8,128)(2,1)S(1)}, u32[]{:S(2)}, u32[]{:S(2)}) collective-permute-start(bf16[64,512]{0,1:T(8,128)(2,1)S(1)} %select_bitcast_fusion), channel_id=1, source_target_pairs={{0,480},{32,0},{64,32},{96,64},{128,96},{160,128},{192,160},{224,1... | collective-permute-start | bytes 196616 | tf_op jit(solution)/shard_map/ppermute | solution.py:26
  159.7 5.6 %collective-permute-start.16 = (bf16[64,512]{0,1:T(8,128)(2,1)S(1)}, bf16[64,512]{0,1:T(8,128)(2,1)S(1)}, u32[]{:S(2)}, u32[]{:S(2)}) collective-permute-start(bf16[64,512]{0,1:T(8,128)(2,1)S(1)} %collective-permute-done.15), channel_id=1, source_target_pairs={{0,32},{32,64},{64,96},{96,128},{128,160},{160,192},{192,224},{224... | collective-permute-start | bytes 196616 | tf_op jit(solution)/shard_map/ppermute | solution.py:24
  159.7 5.8 %collective-permute-start.24 = (bf16[64,512]{0,1:T(8,128)(2,1)S(1)}, bf16[64,512]{0,1:T(8,128)(2,1)S(1)}, u32[]{:S(2)}, u32[]{:S(2)}) collective-permute-start(bf16[64,512]{0,1:T(8,128)(2,1)S(1)} %collective-permute-done.23), channel_id=1, source_target_pairs={{0,480},{32,0},{64,32},{96,64},{128,96},{160,128},{192,160},{224,1... | collective-permute-start | bytes 196616 | tf_op jit(solution)/shard_map/ppermute | solution.py:26
  165.3 5.6 %collective-permute-start.17 = (bf16[64,512]{0,1:T(8,128)(2,1)S(1)}, bf16[64,512]{0,1:T(8,128)(2,1)S(1)}, u32[]{:S(2)}, u32[]{:S(2)}) collective-permute-start(bf16[64,512]{0,1:T(8,128)(2,1)S(1)} %collective-permute-done.16), channel_id=1, source_target_pairs={{0,32},{32,64},{64,96},{96,128},{128,160},{160,192},{192,224},{224... | collective-permute-start | bytes 196616 | tf_op jit(solution)/shard_map/ppermute | solution.py:24
  165.5 42.1 %collective-permute-start.25 = (bf16[64,512]{0,1:T(8,128)(2,1)S(1)}, bf16[64,512]{0,1:T(8,128)(2,1)S(1)}, u32[]{:S(2)}, u32[]{:S(2)}) collective-permute-start(bf16[64,512]{0,1:T(8,128)(2,1)S(1)} %collective-permute-done.24), channel_id=1, source_target_pairs={{0,480},{32,0},{64,32},{96,64},{128,96},{160,128},{192,160},{224,1... | collective-permute-start | bytes 196616 | tf_op jit(solution)/shard_map/ppermute | solution.py:26
  170.9 37.7 %collective-permute-start.18 = (bf16[64,512]{0,1:T(8,128)(2,1)S(1)}, bf16[64,512]{0,1:T(8,128)(2,1)S(1)}, u32[]{:S(2)}, u32[]{:S(2)}) collective-permute-start(bf16[64,512]{0,1:T(8,128)(2,1)S(1)} %collective-permute-done.17), channel_id=1, source_target_pairs={{0,32},{32,64},{64,96},{96,128},{128,160},{160,192},{192,224},{224... | collective-permute-start | bytes 196616 | tf_op jit(solution)/shard_map/ppermute | solution.py:24
  200.0 28.9 %copy-start.2 = (f32[144,64]{0,1:T(8,128)}, f32[144,64]{0,1:T(8,128)S(1)}, u32[]{:S(2)}) copy-start(f32[144,64]{0,1:T(8,128)S(1)} %reduce_sum.85) | copy-start | bytes 110596
  201.2 39.5 %all-to-all-start.2 = ((bf16[32,144,64]{1,2,0:T(8,128)(2,1)}), bf16[32,144,64]{1,2,0:T(8,128)(2,1)}, u32[]{:S(2)}, u32[]{:S(2)}) async-start(bf16[32,144,64]{1,2,0:T(8,128)(2,1)} %broadcast_in_dim.20), calls=%async_computation.2 | async-start | bytes 2097152 | tf_op jit(solution)/shard_map/all_to_all | solution.py:38
  207.5 80.5 %all-gather.7.cloned.1.call-start = ((), (), s32[]{:S(2)}) async-start(), calls=%async_computation.5 | async-start | bytes 5013504 | tf_op jit(solution)/shard_map/all_gather | solution.py:55
  207.6 3.5 collective-permute-start.26
  208.6 5.8 %collective-permute-start.19 = (bf16[64,512]{0,1:T(8,128)(2,1)S(1)}, bf16[64,512]{0,1:T(8,128)(2,1)S(1)}, u32[]{:S(2)}, u32[]{:S(2)}) collective-permute-start(bf16[64,512]{0,1:T(8,128)(2,1)S(1)} %collective-permute-done.18), channel_id=1, source_target_pairs={{0,32},{32,64},{64,96},{96,128},{128,160},{160,192},{192,224},{224... | collective-permute-start | bytes 196616 | tf_op jit(solution)/shard_map/ppermute | solution.py:24
  211.1 5.8 %collective-permute-start.27 = (bf16[64,512]{0,1:T(8,128)(2,1)S(1)}, bf16[64,512]{0,1:T(8,128)(2,1)S(1)}, u32[]{:S(2)}, u32[]{:S(2)}) collective-permute-start(bf16[64,512]{0,1:T(8,128)(2,1)S(1)} %collective-permute-done.26), channel_id=1, source_target_pairs={{0,480},{32,0},{64,32},{96,64},{128,96},{160,128},{192,160},{224,1... | collective-permute-start | bytes 196616 | tf_op jit(solution)/shard_map/ppermute | solution.py:26
  214.4 6.0 %collective-permute-start.20 = (bf16[64,512]{0,1:T(8,128)(2,1)S(1)}, bf16[64,512]{0,1:T(8,128)(2,1)S(1)}, u32[]{:S(2)}, u32[]{:S(2)}) collective-permute-start(bf16[64,512]{0,1:T(8,128)(2,1)S(1)} %collective-permute-done.19), channel_id=1, source_target_pairs={{0,32},{32,64},{64,96},{96,128},{128,160},{160,192},{192,224},{224... | collective-permute-start | bytes 196616 | tf_op jit(solution)/shard_map/ppermute | solution.py:24
  217.0 6.0 %collective-permute-start.28 = (bf16[64,512]{0,1:T(8,128)(2,1)S(1)}, bf16[64,512]{0,1:T(8,128)(2,1)S(1)}, u32[]{:S(2)}, u32[]{:S(2)}) collective-permute-start(bf16[64,512]{0,1:T(8,128)(2,1)S(1)} %collective-permute-done.27), channel_id=1, source_target_pairs={{0,480},{32,0},{64,32},{96,64},{128,96},{160,128},{192,160},{224,1... | collective-permute-start | bytes 196616 | tf_op jit(solution)/shard_map/ppermute | solution.py:26
  220.4 6.0 %collective-permute-start.21 = (bf16[64,512]{0,1:T(8,128)(2,1)S(1)}, bf16[64,512]{0,1:T(8,128)(2,1)S(1)}, u32[]{:S(2)}, u32[]{:S(2)}) collective-permute-start(bf16[64,512]{0,1:T(8,128)(2,1)S(1)} %collective-permute-done.20), channel_id=1, source_target_pairs={{0,32},{32,64},{64,96},{96,128},{128,160},{160,192},{192,224},{224... | collective-permute-start | bytes 196616 | tf_op jit(solution)/shard_map/ppermute | solution.py:24
  223.0 6.0 %collective-permute-start.29 = (bf16[64,512]{0,1:T(8,128)(2,1)S(1)}, bf16[64,512]{0,1:T(8,128)(2,1)S(1)}, u32[]{:S(2)}, u32[]{:S(2)}) collective-permute-start(bf16[64,512]{0,1:T(8,128)(2,1)S(1)} %collective-permute-done.28), channel_id=1, source_target_pairs={{0,480},{32,0},{64,32},{96,64},{128,96},{160,128},{192,160},{224,1... | collective-permute-start | bytes 196616 | tf_op jit(solution)/shard_map/ppermute | solution.py:26
  226.4 5.6 %collective-permute-start.22 = (bf16[64,512]{0,1:T(8,128)(2,1)S(1)}, bf16[64,512]{0,1:T(8,128)(2,1)S(1)}, u32[]{:S(2)}, u32[]{:S(2)}) collective-permute-start(bf16[64,512]{0,1:T(8,128)(2,1)S(1)} %collective-permute-done.21), channel_id=1, source_target_pairs={{0,32},{32,64},{64,96},{96,128},{128,160},{160,192},{192,224},{224... | collective-permute-start | bytes 196616 | tf_op jit(solution)/shard_map/ppermute | solution.py:24
  240.7 50.2 %copy-start.1 = (bf16[512,2048]{1,0:T(8,128)(2,1)}, bf16[512,2048]{1,0:T(8,128)(2,1)S(1)}, u32[]{:S(2)}) copy-start(bf16[512,2048]{1,0:T(8,128)(2,1)S(1)} %exponential_convert_fusion) | copy-start | bytes 6291460
  357.9 0.8 copy-start.3
  357.9 0.9 copy-start.5
Sparse Core Ops, SparseCore 0:
  86.6 44.0 all-gather.4
  244.4 43.5 all-gather.6
